TPU v7x, 32 devices: a whole 2x2x4 slice. The times are simulated.
32 devices in a mesh: gx: 8 (over z, y), gy: 4 (over x, core).
Axes of the slice: x: 2, y: 2, z: 4, core: 2. Of those that a mesh axis runs over, the one named last changes fastest.
Arguments:
- point_feats: bfloat16 [32, 262144], P(None, ('gx', 'gy')), may hold values from -1 to 1
- point_targets: bfloat16 [262144], P(('gx', 'gy')), may hold values from -6 to 6
- point_lists: int32 [32768, 8], P(('gx', 'gy')), may hold values from -1 to 8191, as said below
- brick_adjacency: int32 [1024, 4], P(('gx', 'gy')), may hold values from -1 to 1023, as said below
- voxel_feats: float32 [1024, 32, 512], P(('gx', 'gy')), may hold values from -0.25 to 0.25
- voxel_reg: float32 [1024, 512], P(('gx', 'gy')), may hold values from 0.25 to 2
Outputs:
- solution: float32 [1024, 512], P(('gx', 'gy'))
- residual: float32 [1024, 512], P(('gx', 'gy'))
Inputs may be any that keep to these rules, and one draw needn't show every extreme that they name: `point_lists`: row s * 1024 + b lists, in its first slots, distinct indices of the points of source device s in brick b, all within that device's rows b * 8 to b * 8 + 7, then -1 in the remaining slots. Point rows named by no list are unused. `brick_adjacency`: entry k of brick b is the lattice neighbour of b in direction k (minus along the road, plus along the road, minus across, plus across) or -1; the relation is symmetric and -1 wherever the neighbour lies outside the lattice.
All inputs are finite; a program needn't handle non-finite values.
Results may differ from a plain program's by a relative error of at most 0.0003.
Values may be sent and summed in bfloat16 or wider, within the bound.
A program may use at most 64 MiB of HBM per device.

v0:
```python
import jax
import jax.numpy as jnp
from jax import lax
from jax.sharding import PartitionSpec as P

BX = 8
BY = 4
ITERS = 3
coupling_weight = 1.0


def extended(block, sides, width):
    for axis, dim in sides:
        count = lax.axis_size(axis)
        forward = [(i, i + 1) for i in range(count - 1)]
        backward = [(target, source) for source, target in forward]
        low = lax.ppermute(
            lax.slice_in_dim(block, block.shape[dim] - width, None, axis=dim), axis, forward
        )
        high = lax.ppermute(lax.slice_in_dim(block, 0, width, axis=dim), axis, backward)
        block = jnp.concatenate([low, block, high], axis=dim)
    return block


def neighbour_sum(padded, mask):
    total = mask[..., 0:1] * padded[:-2, 1:-1] + mask[..., 1:2] * padded[2:, 1:-1]
    return total + mask[..., 2:3] * padded[1:-1, :-2] + mask[..., 3:4] * padded[1:-1, 2:]


def shards(point_feats, point_targets, point_lists, brick_adjacency, voxel_feats, voxel_reg):
    feat_count = point_feats.shape[0]
    brick_total, slots = point_lists.shape
    local_bricks = voxel_feats.shape[0]
    devices = brick_total // local_bricks
    live = point_lists >= 0
    offset = point_lists - jnp.arange(brick_total, dtype=jnp.int32)[:, None] * slots
    choose = (offset[:, :, None] == jnp.arange(slots, dtype=jnp.int32)[None, None, :]) & live[
        :, :, None
    ]
    choose = choose.astype(jnp.bfloat16)
    blocks = point_feats.reshape(feat_count, brick_total, slots)
    picked = jnp.einsum("ibd,bcd->ibc", blocks, choose, preferred_element_type=jnp.float32).astype(
        jnp.bfloat16
    )
    target_blocks = point_targets.reshape(brick_total, slots)
    targets = jnp.einsum(
        "bd,bcd->bc", target_blocks, choose, preferred_element_type=jnp.float32
    ).astype(jnp.bfloat16)
    sending = picked.reshape(feat_count, devices, local_bricks * slots)
    target_rows = targets.reshape(1, devices, local_bricks * slots)
    got_feats, got_targets = (
        lax.all_to_all(sending, ("gx", "gy"), split_axis=1, concat_axis=1, tiled=True),
        lax.all_to_all(target_rows, ("gx", "gy"), split_axis=1, concat_axis=1, tiled=True),
    )
    got_feats = got_feats.reshape(feat_count, devices, local_bricks, slots)
    got_targets = got_targets.reshape(devices, local_bricks, slots)
    moments = jnp.einsum("isbc,jsbc->bij", got_feats, got_feats, preferred_element_type=jnp.float32)
    gathered = jnp.einsum(
        "sbc,isbc->bi", got_targets, got_feats, preferred_element_type=jnp.float32
    )
    mask = (brick_adjacency >= 0).astype(jnp.float32).reshape(BX, BY, 4)
    degree = jnp.sum(mask, axis=-1, keepdims=True)

    def operate(vector):
        projected = jnp.einsum("bik,bk->bi", voxel_feats, vector, precision=lax.Precision.HIGHEST)
        lattice = projected.reshape(BX, BY, feat_count)
        padded = extended(lattice, (("gx", 0), ("gy", 1)), 1)
        coupled = (degree * lattice - neighbour_sum(padded, mask)).reshape(local_bricks, feat_count)
        middle = jnp.einsum("bij,bj->bi", moments, projected, precision=lax.Precision.HIGHEST)
        middle = middle + coupling_weight * coupled
        back = jnp.einsum("bik,bi->bk", voxel_feats, middle, precision=lax.Precision.HIGHEST)
        return back + voxel_reg * vector

    def two_products(values, image):
        return lax.psum((jnp.sum(values * values), jnp.sum(values * image)), ("gx", "gy"))

    rhs = jnp.einsum("bik,bi->bk", voxel_feats, gathered, precision=lax.Precision.HIGHEST)
    solution = jnp.zeros_like(rhs)
    residual = rhs
    image = operate(residual)
    norm_now, product = two_products(residual, image)
    alpha = norm_now / product
    direction, carried = (residual, image)
    for iteration in range(ITERS):
        solution = solution + alpha * direction
        residual = residual - alpha * carried
        if iteration + 1 < ITERS:
            image = operate(residual)
            norm_next, product = two_products(residual, image)
            ratio = norm_next / norm_now
            alpha = norm_next / (product - ratio * norm_next / alpha)
            direction = residual + ratio * direction
            carried = image + ratio * carried
            norm_now = norm_next
    return (solution, residual)


def solution(mesh):
    placed = (
        P(None, ("gx", "gy")),
        P(("gx", "gy")),
        P(("gx", "gy"), None),
        P(("gx", "gy"), None),
        P(("gx", "gy"), None, None),
        P(("gx", "gy"), None),
    )
    return jax.shard_map(
        shards,
        mesh=mesh,
        in_specs=placed,
        out_specs=(P(("gx", "gy"), None), P(("gx", "gy"), None)),
        check_vma=False,
    )
```

profile of v0, /device:TPU:0, one launch (start us, length us, event | category | flops | bytes accessed | tf_op | source)
XLA Modules:
  0.0 251.1 jit_solution(11795975120160489143)
XLA Ops:
  0.7 0.9 broadcast_compare_fusion
  1.6 0.8 broadcast_subtract_fusion
  2.8 2.1 reshape.98
  4.9 5.8 %fusion.3 = f32[1024,1,8]{2,1,0:T(1,128)S(1)} fusion(bf16[1024,8,1]{1,2,0:T(2,128)(2,1)} %reshape.98, s32[1024,8]{1,0:T(8,128)S(1)} %copy.33, pred[1024,8]{1,0:T(8,128)(4,1)S(1)} %copy.34), kind=kOutput, calls=%fused_computation.3 | convolution fusion | flops 262144 | bytes 90112 | tf_op jit(solution)/shard_map/bd,bcd->bc/dot_general | solution.py:46
  11.6 0.7 reduce.1
  12.9 7.3 %all-to-all-start = ((bf16[32,2,128]{2,1,0:T(2,128)(2,1)}), bf16[32,2,128]{2,1,0:T(2,128)(2,1)S(1)}, u32[]{:S(2)}, u32[]{:S(2)}) async-start(bf16[32,2,128]{2,1,0:T(2,128)(2,1)} %reshape.100), calls=%async_computation | async-start | bytes 32768 | tf_op jit(solution)/shard_map/all_to_all | solution.py:53
  20.3 1.8 copy.37
  22.1 7.1 %fusion.10 = bf16[1024,8,32]{2,1,0:T(8,128)(2,1)} fusion(bf16[32,8192]{0,1:T(8,128)(2,1)} %copy.37, s32[1024,8]{1,0:T(8,128)S(1)} %copy.33, pred[1024,8]{1,0:T(8,128)(4,1)S(1)} %copy-done.5), kind=kOutput, calls=%fused_computation.9 | convolution fusion | flops 4587520 | bytes 1089536 | tf_op jit(solution)/shard_map/ibd,bcd->ibc/dot_general | solution.py:42
  29.2 2.6 %copy.38 = bf16[32,32,256]{2,0,1:T(8,128)(2,1)} copy(bf16[32,32,256]{0,2,1:T(8,128)(2,1)} %bitcast.158) | data formatting | bytes 1048576 | tf_op jit(solution)/shard_map/reshape | solution.py:49
  31.8 5.8 %all-to-all-start.1 = ((bf16[32,32,256]{2,0,1:T(8,128)(2,1)}), bf16[32,32,256]{2,0,1:T(8,128)(2,1)S(1)}, u32[]{:S(2)}, u32[]{:S(2)}) async-start(bf16[32,32,256]{2,0,1:T(8,128)(2,1)} %copy.38), calls=%async_computation.1 | async-start | bytes 1048576 | tf_op jit(solution)/shard_map/all_to_all | solution.py:52
  38.0 15.3 %all-to-all-done.1 = bf16[32,32,256]{2,0,1:T(8,128)(2,1)S(1)} async-done(((bf16[32,32,256]{2,0,1:T(8,128)(2,1)}), bf16[32,32,256]{2,0,1:T(8,128)(2,1)S(1)}, u32[]{:S(2)}, u32[]{:S(2)}) %all-to-all-start.1) | async-done | bytes 524320 | tf_op jit(solution)/shard_map/all_to_all | solution.py:52
  53.2 3.9 %copy.39 = bf16[32,32,256]{1,0,2:T(8,128)(2,1)} copy(bf16[32,32,256]{2,0,1:T(8,128)(2,1)S(1)} %all-to-all-done.1) | data formatting | bytes 1048576 | tf_op jit(solution)/shard_map/all_to_all | solution.py:52
  57.2 2.2 convolution_bitcast_fusion.1
  59.4 1.1 fusion.58
  60.5 1.8 fusion.25
  62.4 3.1 %collective-permute-start = (f32[1,4,32]{2,1,0:T(4,128)S(1)}, f32[1,4,32]{2,1,0:T(4,128)S(1)}, u32[]{:S(2)}, u32[]{:S(2)}) collective-permute-start(f32[1,4,32]{2,1,0:T(4,128)S(1)} %get-tuple-element.31), channel_id=1, source_target_pairs={{0,4},{4,8},{8,12},{12,16},{16,20},{20,24},{24,28},{1,5},{5,9},{9,... | collective-permute-start | bytes 1544 | tf_op jit(solution)/shard_map/ppermute | solution.py:17
  65.5 1.3 collective-permute-start.1
  66.8 0.7 convolution_bitcast_fusion
  67.5 3.5 %collective-permute-done.1 = f32[1,4,32]{2,1,0:T(4,128)S(1)} collective-permute-done((f32[1,4,32]{2,1,0:T(4,128)S(1)}, f32[1,4,32]{2,1,0:T(4,128)S(1)}, u32[]{:S(2)}, u32[]{:S(2)}) %collective-permute-start.1) | collective-permute-done | bytes 544 | tf_op jit(solution)/shard_map/ppermute | solution.py:20
  71.0 1.3 collective-permute-start.2
  72.3 1.3 collective-permute-start.3
  73.6 0.9 fusion.55
  74.5 2.2 collective-permute-done.3
  76.8 1.1 fusion.59
  77.9 0.6 fusion.18
  78.6 40.8 %all-reduce.2 = (f32[]{:T(128)}, f32[]{:T(128)}) all-reduce(f32[]{:T(128)} %get-tuple-element.7, f32[]{:T(128)} %get-tuple-element.6), channel_id=1, replica_groups=mesh['gx'=8,'gy'=4] {'gx','gy'}, use_global_device_ids=true, to_apply=%region_1.0 | all-reduce | flops 2 | bytes 16 | tf_op jit(solution)/shard_map/psum | solution.py:75
  120.7 1.8 fusion.23
  122.5 4.4 %collective-permute-start.4 = (f32[1,4,32]{2,1,0:T(4,128)S(1)}, f32[1,4,32]{2,1,0:T(4,128)S(1)}, u32[]{:S(2)}, u32[]{:S(2)}) collective-permute-start(f32[1,4,32]{2,1,0:T(4,128)S(1)} %get-tuple-element.25), channel_id=1, source_target_pairs={{0,4},{4,8},{8,12},{12,16},{16,20},{20,24},{24,28},{1,5},{5,9},{9,... | collective-permute-start | bytes 1544 | tf_op jit(solution)/shard_map/ppermute | solution.py:17
  126.9 1.3 collective-permute-start.5
  128.2 4.2 %collective-permute-done.5 = f32[1,4,32]{2,1,0:T(4,128)S(1)} collective-permute-done((f32[1,4,32]{2,1,0:T(4,128)S(1)}, f32[1,4,32]{2,1,0:T(4,128)S(1)}, u32[]{:S(2)}, u32[]{:S(2)}) %collective-permute-start.5) | collective-permute-done | bytes 544 | tf_op jit(solution)/shard_map/ppermute | solution.py:20
  132.4 1.3 collective-permute-start.6
  133.7 1.3 collective-permute-start.7
  135.0 0.9 fusion.53
  135.9 1.4 collective-permute-done.7
  137.5 1.1 fusion.60
  138.6 0.6 multiply_reduce_fusion.2
  139.2 41.8 %all-reduce.1 = (f32[]{:T(128)}, f32[]{:T(128)}) all-reduce(f32[]{:T(128)} %get-tuple-element.5, f32[]{:T(128)} %get-tuple-element.4), channel_id=1, replica_groups=mesh['gx'=8,'gy'=4] {'gx','gy'}, use_global_device_ids=true, to_apply=%region_6.0 | all-reduce | flops 2 | bytes 16 | tf_op jit(solution)/shard_map/psum | solution.py:75
  185.7 1.8 fusion.21
  187.5 4.4 %collective-permute-start.8 = (f32[1,4,32]{2,1,0:T(4,128)S(1)}, f32[1,4,32]{2,1,0:T(4,128)S(1)}, u32[]{:S(2)}, u32[]{:S(2)}) collective-permute-start(f32[1,4,32]{2,1,0:T(4,128)S(1)} %get-tuple-element.23), channel_id=1, source_target_pairs={{0,4},{4,8},{8,12},{12,16},{16,20},{20,24},{24,28},{1,5},{5,9},{9,... | collective-permute-start | bytes 1544 | tf_op jit(solution)/shard_map/ppermute | solution.py:17
  192.0 1.3 collective-permute-start.9
  193.3 4.2 %collective-permute-done.9 = f32[1,4,32]{2,1,0:T(4,128)S(1)} collective-permute-done((f32[1,4,32]{2,1,0:T(4,128)S(1)}, f32[1,4,32]{2,1,0:T(4,128)S(1)}, u32[]{:S(2)}, u32[]{:S(2)}) %collective-permute-start.9) | collective-permute-done | bytes 544 | tf_op jit(solution)/shard_map/ppermute | solution.py:20
  197.5 1.3 collective-permute-start.10
  198.8 1.3 collective-permute-start.11
  200.1 0.9 fusion.51
  201.0 1.6 collective-permute-done.11
  202.7 1.1 fusion.61
  204.5 41.9 %all-reduce = (f32[]{:T(128)}, f32[]{:T(128)}) all-reduce(f32[]{:T(128)} %get-tuple-element.3, f32[]{:T(128)} %get-tuple-element.2), channel_id=1, replica_groups=mesh['gx'=8,'gy'=4] {'gx','gy'}, use_global_device_ids=true, to_apply=%region_10.0 | all-reduce | flops 2 | bytes 16 | tf_op jit(solution)/shard_map/psum | solution.py:75
  250.4 0.7 multiply_subtract_fusion
  (51 shorter events, 3.3 us)
Async XLA Ops:
  0.6 58.8 %copy-start = (f32[32,32,512]{2,1,0:T(8,128)S(1)}, f32[32,32,512]{2,1,0:T(8,128)}, u32[]{:S(2)}) copy-start(f32[32,32,512]{2,1,0:T(8,128)} %param.10) | copy-start | bytes 6291460
  2.8 8.0 %copy-start.4 = (pred[1024,8]{1,0:T(8,128)(4,1)}, pred[1024,8]{1,0:T(8,128)(4,1)S(1)}, u32[]{:S(2)}) copy-start(pred[1024,8]{1,0:T(8,128)(4,1)S(1)} %copy.34) | copy-start | bytes 24580
  4.9 15.4 %copy-start.3 = (bf16[32,8192]{1,0:T(8,128)(2,1)S(1)}, bf16[32,8192]{1,0:T(8,128)(2,1)}, u32[]{:S(2)}) copy-start(bf16[32,8192]{1,0:T(8,128)(2,1)} %param.6) | copy-start | bytes 1572868
  11.1 11.0 %copy-start.5 = (pred[1024,8]{1,0:T(8,128)(4,1)S(1)}, pred[1024,8]{1,0:T(8,128)(4,1)}, u32[]{:S(2)}) copy-start(pred[1024,8]{1,0:T(8,128)(4,1)} %copy-done.4) | copy-start | bytes 24580
  12.9 18.8 %all-to-all-start = ((bf16[32,2,128]{2,1,0:T(2,128)(2,1)}), bf16[32,2,128]{2,1,0:T(2,128)(2,1)S(1)}, u32[]{:S(2)}, u32[]{:S(2)}) async-start(bf16[32,2,128]{2,1,0:T(2,128)(2,1)} %reshape.100), calls=%async_computation | async-start | bytes 32768 | tf_op jit(solution)/shard_map/all_to_all | solution.py:53
  29.2 8.4 %copy-start.6 = (s32[32,4]{0,1:T(4,128)S(1)}, s32[32,4]{0,1:T(4,128)}, u32[]{:S(2)}) copy-start(s32[32,4]{0,1:T(4,128)} %param.9) | copy-start | bytes 1540
  31.8 21.5 %all-to-all-start.1 = ((bf16[32,32,256]{2,0,1:T(8,128)(2,1)}), bf16[32,32,256]{2,0,1:T(8,128)(2,1)S(1)}, u32[]{:S(2)}, u32[]{:S(2)}) async-start(bf16[32,32,256]{2,0,1:T(8,128)(2,1)} %copy.38), calls=%async_computation.1 | async-start | bytes 1048576 | tf_op jit(solution)/shard_map/all_to_all | solution.py:52
  59.4 7.4 %copy-start.1 = (bf16[32,32,256]{1,0,2:T(8,128)(2,1)S(1)}, bf16[32,32,256]{1,0,2:T(8,128)(2,1)}, u32[]{:S(2)}) copy-start(bf16[32,32,256]{1,0,2:T(8,128)(2,1)} %copy.39) | copy-start | bytes 1572868
  62.4 5.1 %collective-permute-start = (f32[1,4,32]{2,1,0:T(4,128)S(1)}, f32[1,4,32]{2,1,0:T(4,128)S(1)}, u32[]{:S(2)}, u32[]{:S(2)}) collective-permute-start(f32[1,4,32]{2,1,0:T(4,128)S(1)} %get-tuple-element.31), channel_id=1, source_target_pairs={{0,4},{4,8},{8,12},{12,16},{16,20},{20,24},{24,28},{1,5},{5,9},{9,... | collective-permute-start | bytes 1544 | tf_op jit(solution)/shard_map/ppermute | solution.py:17
  65.5 5.5 %collective-permute-start.1 = (f32[1,4,32]{2,1,0:T(4,128)S(1)}, f32[1,4,32]{2,1,0:T(4,128)S(1)}, u32[]{:S(2)}, u32[]{:S(2)}) collective-permute-start(f32[1,4,32]{2,1,0:T(4,128)S(1)} %get-tuple-element.32), channel_id=1, source_target_pairs={{4,0},{8,4},{12,8},{16,12},{20,16},{24,20},{28,24},{5,1},{9,5},{13... | collective-permute-start | bytes 1544 | tf_op jit(solution)/shard_map/ppermute | solution.py:20
  67.4 10.5 %copy-start.2 = (f32[32,512]{1,0:T(8,128)S(1)}, f32[32,512]{1,0:T(8,128)}, u32[]{:S(2)}) copy-start(f32[32,512]{1,0:T(8,128)} %param.11) | copy-start | bytes 196612
  71.0 3.5 %collective-permute-start.2 = (f32[10,1,32]{2,1,0:T(1,128)S(1)}, f32[10,1,32]{2,1,0:T(1,128)S(1)}, u32[]{:S(2)}, u32[]{:S(2)}) collective-permute-start(f32[10,1,32]{2,1,0:T(1,128)S(1)} %get-tuple-element.21), channel_id=1, source_target_pairs={{0,1},{1,2},{2,3},{4,5},{5,6},{6,7},{8,9},{9,10},{10,11},{12,13},{... | collective-permute-start | bytes 3848 | tf_op jit(solution)/shard_map/ppermute | solution.py:17
  72.3 4.4 %collective-permute-start.3 = (f32[10,1,32]{2,1,0:T(1,128)S(1)}, f32[10,1,32]{2,1,0:T(1,128)S(1)}, u32[]{:S(2)}, u32[]{:S(2)}) collective-permute-start(f32[10,1,32]{2,1,0:T(1,128)S(1)} %get-tuple-element.22), channel_id=1, source_target_pairs={{1,0},{2,1},{3,2},{5,4},{6,5},{7,6},{9,8},{10,9},{11,10},{13,12},{... | collective-permute-start | bytes 3848 | tf_op jit(solution)/shard_map/ppermute | solution.py:20
  122.5 5.7 %collective-permute-start.4 = (f32[1,4,32]{2,1,0:T(4,128)S(1)}, f32[1,4,32]{2,1,0:T(4,128)S(1)}, u32[]{:S(2)}, u32[]{:S(2)}) collective-permute-start(f32[1,4,32]{2,1,0:T(4,128)S(1)} %get-tuple-element.25), channel_id=1, source_target_pairs={{0,4},{4,8},{8,12},{12,16},{16,20},{20,24},{24,28},{1,5},{5,9},{9,... | collective-permute-start | bytes 1544 | tf_op jit(solution)/shard_map/ppermute | solution.py:17
  126.9 5.5 %collective-permute-start.5 = (f32[1,4,32]{2,1,0:T(4,128)S(1)}, f32[1,4,32]{2,1,0:T(4,128)S(1)}, u32[]{:S(2)}, u32[]{:S(2)}) collective-permute-start(f32[1,4,32]{2,1,0:T(4,128)S(1)} %get-tuple-element.26), channel_id=1, source_target_pairs={{4,0},{8,4},{12,8},{16,12},{20,16},{24,20},{28,24},{5,1},{9,5},{13... | collective-permute-start | bytes 1544 | tf_op jit(solution)/shard_map/ppermute | solution.py:20
  132.4 3.5 %collective-permute-start.6 = (f32[10,1,32]{2,1,0:T(1,128)S(1)}, f32[10,1,32]{2,1,0:T(1,128)S(1)}, u32[]{:S(2)}, u32[]{:S(2)}) collective-permute-start(f32[10,1,32]{2,1,0:T(1,128)S(1)} %get-tuple-element.19), channel_id=1, source_target_pairs={{0,1},{1,2},{2,3},{4,5},{5,6},{6,7},{8,9},{9,10},{10,11},{12,13},{... | collective-permute-start | bytes 3848 | tf_op jit(solution)/shard_map/ppermute | solution.py:17
  133.7 3.7 %collective-permute-start.7 = (f32[10,1,32]{2,1,0:T(1,128)S(1)}, f32[10,1,32]{2,1,0:T(1,128)S(1)}, u32[]{:S(2)}, u32[]{:S(2)}) collective-permute-start(f32[10,1,32]{2,1,0:T(1,128)S(1)} %get-tuple-element.20), channel_id=1, source_target_pairs={{1,0},{2,1},{3,2},{5,4},{6,5},{7,6},{9,8},{10,9},{11,10},{13,12},{... | collective-permute-start | bytes 3848 | tf_op jit(solution)/shard_map/ppermute | solution.py:20
  187.5 5.8 %collective-permute-start.8 = (f32[1,4,32]{2,1,0:T(4,128)S(1)}, f32[1,4,32]{2,1,0:T(4,128)S(1)}, u32[]{:S(2)}, u32[]{:S(2)}) collective-permute-start(f32[1,4,32]{2,1,0:T(4,128)S(1)} %get-tuple-element.23), channel_id=1, source_target_pairs={{0,4},{4,8},{8,12},{12,16},{16,20},{20,24},{24,28},{1,5},{5,9},{9,... | collective-permute-start | bytes 1544 | tf_op jit(solution)/shard_map/ppermute | solution.py:17
  192.0 5.5 %collective-permute-start.9 = (f32[1,4,32]{2,1,0:T(4,128)S(1)}, f32[1,4,32]{2,1,0:T(4,128)S(1)}, u32[]{:S(2)}, u32[]{:S(2)}) collective-permute-start(f32[1,4,32]{2,1,0:T(4,128)S(1)} %get-tuple-element.24), channel_id=1, source_target_pairs={{4,0},{8,4},{12,8},{16,12},{20,16},{24,20},{28,24},{5,1},{9,5},{13... | collective-permute-start | bytes 1544 | tf_op jit(solution)/shard_map/ppermute | solution.py:20
  197.5 3.5 %collective-permute-start.10 = (f32[10,1,32]{2,1,0:T(1,128)S(1)}, f32[10,1,32]{2,1,0:T(1,128)S(1)}, u32[]{:S(2)}, u32[]{:S(2)}) collective-permute-start(f32[10,1,32]{2,1,0:T(1,128)S(1)} %get-tuple-element.17), channel_id=1, source_target_pairs={{0,1},{1,2},{2,3},{4,5},{5,6},{6,7},{8,9},{9,10},{10,11},{12,13},{... | collective-permute-start | bytes 3848 | tf_op jit(solution)/shard_map/ppermute | solution.py:17
  198.8 3.8 %collective-permute-start.11 = (f32[10,1,32]{2,1,0:T(1,128)S(1)}, f32[10,1,32]{2,1,0:T(1,128)S(1)}, u32[]{:S(2)}, u32[]{:S(2)}) collective-permute-start(f32[10,1,32]{2,1,0:T(1,128)S(1)} %get-tuple-element.18), channel_id=1, source_target_pairs={{1,0},{2,1},{3,2},{5,4},{6,5},{7,6},{9,8},{10,9},{11,10},{13,12},{... | collective-permute-start | bytes 3848 | tf_op jit(solution)/shard_map/ppermute | solution.py:20
where the time goes:
time: 252 us; the launch traced here: 251 us
  blocking collectives  124 us (49%)
  starting transfers between devices  36.7 us (15%)
  waiting for transfers between devices  32.3 us (13%)
  matrix products  28.5 us (11%)
  local copies, waits for them, and re-layouts  12.6 us (5%)
  between operations  11.1 us (4%)
  other arithmetic  5.47 us (2%)
    psum x3, blocking collectives, two_products(): lax.psum((jnp.sum(values * values), jnp.sum(values * image)), ('gx', 'gy'))  124 us
    ppermute x6, waiting for transfers between devices, extended(): lax.ppermute(lax.slice_in_dim(block, 0, width, axis=dim), axis, backward)  17 us
    ppermute x6, starting transfers between devices, extended(): lax.ppermute(lax.slice_in_dim(block, block.shape[dim] - width, None, axis...  15.8 us
    all_to_all x1, waiting for transfers between devices, shards(): lax.all_to_all(sending, ('gx', 'gy'), split_axis=1, concat_axis=1, tiled=...  15.3 us
    ppermute x6, starting transfers between devices, extended(): lax.ppermute(lax.slice_in_dim(block, 0, width, axis=dim), axis, backward)  7.75 us
    all_to_all x1, starting transfers between devices, shards(): lax.all_to_all(target_rows, ('gx', 'gy'), split_axis=1, concat_axis=1, ti...  7.33 us
    dot_general x1, matrix products, shards(): jnp.einsum('ibd,bcd->ibc', blocks, choose, preferred_element_type=jnp.flo...  7.12 us
    dot_general x1, matrix products, shards(): jnp.einsum('bd,bcd->bc', target_blocks, choose, preferred_element_type=jn...  5.85 us
  transfers between devices with their start and end apart: 14, of which 7 were waited for; matrix products, arithmetic and copies ran while one was open for 6% of the time, Pallas kernels for 0%

commit v1 on v0

--- a/solution.py
+++ b/solution.py
@@ -49,7 +49,15 @@
     sending = picked.reshape(feat_count, devices, local_bricks * slots)
     target_rows = targets.reshape(1, devices, local_bricks * slots)
     got_feats, got_targets = (
-        lax.all_to_all(sending, ("gx", "gy"), split_axis=1, concat_axis=1, tiled=True),
+        jnp.concatenate(
+            lax.all_to_all(
+                jnp.stack(jnp.split(sending, lax.axis_size(("gx", "gy")), axis=1)),
+                ("gx", "gy"),
+                0,
+                0,
+            ),
+            axis=1,
+        ),
         lax.all_to_all(target_rows, ("gx", "gy"), split_axis=1, concat_axis=1, tiled=True),
     )
     got_feats = got_feats.reshape(feat_count, devices, local_bricks, slots)

time: 252 us -> 296 us (1.17)
  local copies, waits for them, and re-layouts: 12.6 us -> 55.8 us
    unnamed x18 -> x81, local copies, waits for them, and re-layouts: 2.95 us -> 47.2 us
    all_to_all x1 -> x0, local copies, waits for them, and re-layouts: 3.94 us -> none  [shards(): lax.all_to_all(sending, ('gx', 'gy'), split_axis=1, concat_axis=1, tiled=...]
  transfers between devices with their start and end apart: 14 -> 14, of which waited for: 7 -> 7; matrix products, arithmetic and copies ran while one was open for 6% -> 20% of each run, Pallas kernels for 0% -> 0%
where the time goes in v1:
time: 296 us; the launch traced here: 293 us
  blocking collectives  124 us (42%)
  local copies, waits for them, and re-layouts  55.8 us (19%)
  starting transfers between devices  36.9 us (12%)
  waiting for transfers between devices  32.1 us (11%)
  matrix products  27.5 us (9%)
  between operations  11.1 us (4%)
  other arithmetic  5.54 us (2%)
    psum x3, blocking collectives, two_products(): lax.psum((jnp.sum(values * values), jnp.sum(values * image)), ('gx', 'gy'))  124 us
    unnamed x81, local copies, waits for them, and re-layouts  47.2 us
    ppermute x6, waiting for transfers between devices, extended(): lax.ppermute(lax.slice_in_dim(block, 0, width, axis=dim), axis, backward)  16.9 us
    ppermute x6, starting transfers between devices, extended(): lax.ppermute(lax.slice_in_dim(block, block.shape[dim] - width, None, axis...  15.8 us
    all_to_all x1, waiting for transfers between devices, shards(): lax.all_to_all(jnp.stack(jnp.split(sending, lax.axis_size(('gx', 'gy')),...  15.3 us
    ppermute x6, starting transfers between devices, extended(): lax.ppermute(lax.slice_in_dim(block, 0, width, axis=dim), axis, backward)  7.93 us
    all_to_all x1, starting transfers between devices, shards(): lax.all_to_all(target_rows, ('gx', 'gy'), split_axis=1, concat_axis=1, ti...  7.33 us
    dot_general x1, matrix products, shards(): jnp.einsum('ibd,bcd->ibc', blocks, choose, preferred_element_type=jnp.flo...  6.12 us
  transfers between devices with their start and end apart: 14, of which 7 were waited for; matrix products, arithmetic and copies ran while one was open for 20% of the time, Pallas kernels for 0%

profile of v1, /device:TPU:0, one launch (start us, length us, event | category | flops | bytes accessed | tf_op | source)
XLA Modules:
  0.0 293.4 jit_solution(17849293042728505420)
XLA Ops:
  2.8 2.1 reshape.98
  4.9 5.8 %fusion.3 = f32[1024,1,8]{2,1,0:T(1,128)S(1)} fusion(bf16[1024,8,1]{1,2,0:T(2,128)(2,1)} %reshape.98, s32[1024,8]{1,0:T(8,128)S(1)} %copy.33, pred[1024,8]{1,0:T(8,128)(4,1)S(1)} %copy.34), kind=kOutput, calls=%fused_computation.3 | convolution fusion | flops 262144 | bytes 90112 | tf_op jit(solution)/shard_map/bd,bcd->bc/dot_general | solution.py:46
  12.9 7.3 %all-to-all-start = ((bf16[32,2,128]{2,1,0:T(2,128)(2,1)}), bf16[32,2,128]{2,1,0:T(2,128)(2,1)S(1)}, u32[]{:S(2)}, u32[]{:S(2)}) async-start(bf16[32,2,128]{2,1,0:T(2,128)(2,1)} %reshape.100), calls=%async_computation | async-start | bytes 32768 | tf_op jit(solution)/shard_map/all_to_all | solution.py:61
  20.3 1.8 copy.37
  22.1 6.1 %fusion.10 = bf16[1024,8,32]{2,1,0:T(8,128)(2,1)S(1)} fusion(bf16[32,8192]{0,1:T(8,128)(2,1)} %copy.37, s32[1024,8]{1,0:T(8,128)S(1)} %copy.33, pred[1024,8]{1,0:T(8,128)(4,1)S(1)} %copy-done.5), kind=kOutput, calls=%fused_computation.9 | convolution fusion | flops 4587520 | bytes 1089536 | tf_op jit(solution)/shard_map/ibd,bcd->ibc/dot_general | solution.py:42
  29.2 1.5 copy.108
  30.7 1.3 constant_dynamic-update-slice_fusion.31
  32.0 1.5 copy.109
  33.5 1.5 copy.110
  35.0 1.5 copy.111
  36.5 1.5 copy.112
  38.1 1.5 copy.113
  39.6 1.5 copy.114
  41.1 1.5 copy.115
  42.6 1.5 copy.116
  44.1 1.5 copy.117
  48.2 1.3 constant_dynamic-update-slice_fusion.30
  49.5 1.3 constant_dynamic-update-slice_fusion.29
  50.8 1.3 constant_dynamic-update-slice_fusion.28
  52.1 1.3 constant_dynamic-update-slice_fusion.27
  53.5 1.3 constant_dynamic-update-slice_fusion.26
  54.8 1.3 constant_dynamic-update-slice_fusion.25
  56.1 1.3 constant_dynamic-update-slice_fusion.24
  57.4 1.3 constant_dynamic-update-slice_fusion.23
  58.7 1.3 constant_dynamic-update-slice_fusion.22
  60.1 1.3 constant_dynamic-update-slice_fusion.21
  74.0 5.8 %all-to-all-start.1 = ((bf16[32,32,1,256]{3,1,2,0:T(8,128)(2,1)}), bf16[32,32,1,256]{3,1,2,0:T(8,128)(2,1)S(1)}, u32[]{:S(2)}, u32[]{:S(2)}) async-start(bf16[32,32,1,256]{3,1,2,0:T(8,128)(2,1)} %constant_dynamic-update-slice_fusion), calls=%async_computation.1 | async-start | bytes 1048576 | tf_op jit(solution)/shard_map/all_to_all | solution.py:53
  80.2 15.3 %all-to-all-done.1 = bf16[32,32,1,256]{3,1,2,0:T(8,128)(2,1)S(1)} async-done(((bf16[32,32,1,256]{3,1,2,0:T(8,128)(2,1)}), bf16[32,32,1,256]{3,1,2,0:T(8,128)(2,1)S(1)}, u32[]{:S(2)}, u32[]{:S(2)}) %all-to-all-start.1) | async-done | bytes 524320 | tf_op jit(solution)/shard_map/all_to_all | solution.py:53
  95.5 4.0 %copy.70 = bf16[32,32,1,256]{1,0,3,2:T(8,128)(2,1)} copy(bf16[32,32,1,256]{3,0,2,1:T(8,128)(2,1)S(1)} %bitcast.223) | data formatting | bytes 1048576 | tf_op jit(solution)/shard_map/reshape | solution.py:52
  99.4 2.2 convolution_bitcast_fusion.1
  102.8 1.8 fusion.25
  104.6 3.1 %collective-permute-start = (f32[1,4,32]{2,1,0:T(4,128)S(1)}, f32[1,4,32]{2,1,0:T(4,128)S(1)}, u32[]{:S(2)}, u32[]{:S(2)}) collective-permute-start(f32[1,4,32]{2,1,0:T(4,128)S(1)} %get-tuple-element.63), channel_id=1, source_target_pairs={{0,4},{4,8},{8,12},{12,16},{16,20},{20,24},{24,28},{1,5},{5,9},{9,... | collective-permute-start | bytes 1544 | tf_op jit(solution)/shard_map/ppermute | solution.py:17
  107.7 1.3 collective-permute-start.1
  109.7 3.5 %collective-permute-done.1 = f32[1,4,32]{2,1,0:T(4,128)S(1)} collective-permute-done((f32[1,4,32]{2,1,0:T(4,128)S(1)}, f32[1,4,32]{2,1,0:T(4,128)S(1)}, u32[]{:S(2)}, u32[]{:S(2)}) %collective-permute-start.1) | collective-permute-done | bytes 544 | tf_op jit(solution)/shard_map/ppermute | solution.py:20
  114.5 1.5 collective-permute-start.3
  116.9 2.0 collective-permute-done.3
  120.8 40.6 %all-reduce.2 = (f32[]{:T(128)}, f32[]{:T(128)}) all-reduce(f32[]{:T(128)} %get-tuple-element.7, f32[]{:T(128)} %get-tuple-element.6), channel_id=1, replica_groups=mesh['gx'=8,'gy'=4] {'gx','gy'}, use_global_device_ids=true, to_apply=%region_1.0 | all-reduce | flops 2 | bytes 16 | tf_op jit(solution)/shard_map/psum | solution.py:83
  162.8 1.8 fusion.23
  164.6 4.4 %collective-permute-start.4 = (f32[1,4,32]{2,1,0:T(4,128)S(1)}, f32[1,4,32]{2,1,0:T(4,128)S(1)}, u32[]{:S(2)}, u32[]{:S(2)}) collective-permute-start(f32[1,4,32]{2,1,0:T(4,128)S(1)} %get-tuple-element.57), channel_id=1, source_target_pairs={{0,4},{4,8},{8,12},{12,16},{16,20},{20,24},{24,28},{1,5},{5,9},{9,... | collective-permute-start | bytes 1544 | tf_op jit(solution)/shard_map/ppermute | solution.py:17
  169.0 1.3 collective-permute-start.5
  170.3 4.2 %collective-permute-done.5 = f32[1,4,32]{2,1,0:T(4,128)S(1)} collective-permute-done((f32[1,4,32]{2,1,0:T(4,128)S(1)}, f32[1,4,32]{2,1,0:T(4,128)S(1)}, u32[]{:S(2)}, u32[]{:S(2)}) %collective-permute-start.5) | collective-permute-done | bytes 544 | tf_op jit(solution)/shard_map/ppermute | solution.py:20
  178.0 1.4 collective-permute-done.7
  181.4 41.9 %all-reduce.1 = (f32[]{:T(128)}, f32[]{:T(128)}) all-reduce(f32[]{:T(128)} %get-tuple-element.5, f32[]{:T(128)} %get-tuple-element.4), channel_id=1, replica_groups=mesh['gx'=8,'gy'=4] {'gx','gy'}, use_global_device_ids=true, to_apply=%region_6.0 | all-reduce | flops 2 | bytes 16 | tf_op jit(solution)/shard_map/psum | solution.py:83
  228.0 1.8 fusion.21
  229.8 4.4 %collective-permute-start.8 = (f32[1,4,32]{2,1,0:T(4,128)S(1)}, f32[1,4,32]{2,1,0:T(4,128)S(1)}, u32[]{:S(2)}, u32[]{:S(2)}) collective-permute-start(f32[1,4,32]{2,1,0:T(4,128)S(1)} %get-tuple-element.55), channel_id=1, source_target_pairs={{0,4},{4,8},{8,12},{12,16},{16,20},{20,24},{24,28},{1,5},{5,9},{9,... | collective-permute-start | bytes 1544 | tf_op jit(solution)/shard_map/ppermute | solution.py:17
  235.5 4.2 %collective-permute-done.9 = f32[1,4,32]{2,1,0:T(4,128)S(1)} collective-permute-done((f32[1,4,32]{2,1,0:T(4,128)S(1)}, f32[1,4,32]{2,1,0:T(4,128)S(1)}, u32[]{:S(2)}, u32[]{:S(2)}) %collective-permute-start.9) | collective-permute-done | bytes 544 | tf_op jit(solution)/shard_map/ppermute | solution.py:20
  243.2 1.6 collective-permute-done.11
  246.7 41.9 %all-reduce = (f32[]{:T(128)}, f32[]{:T(128)}) all-reduce(f32[]{:T(128)} %get-tuple-element.3, f32[]{:T(128)} %get-tuple-element.2), channel_id=1, replica_groups=mesh['gx'=8,'gy'=4] {'gx','gy'}, use_global_device_ids=true, to_apply=%region_10.0 | all-reduce | flops 2 | bytes 16 | tf_op jit(solution)/shard_map/psum | solution.py:83
  (116 shorter events, 39.5 us)
Async XLA Ops:
  0.6 101.0 %copy-start = (f32[32,32,512]{2,1,0:T(8,128)S(1)}, f32[32,32,512]{2,1,0:T(8,128)}, u32[]{:S(2)}) copy-start(f32[32,32,512]{2,1,0:T(8,128)} %param.10) | copy-start | bytes 6291460
  2.8 8.0 %copy-start.4 = (pred[1024,8]{1,0:T(8,128)(4,1)}, pred[1024,8]{1,0:T(8,128)(4,1)S(1)}, u32[]{:S(2)}) copy-start(pred[1024,8]{1,0:T(8,128)(4,1)S(1)} %copy.34) | copy-start | bytes 24580
  4.9 15.4 %copy-start.3 = (bf16[32,8192]{1,0:T(8,128)(2,1)S(1)}, bf16[32,8192]{1,0:T(8,128)(2,1)}, u32[]{:S(2)}) copy-start(bf16[32,8192]{1,0:T(8,128)(2,1)} %param.6) | copy-start | bytes 1572868
  11.1 11.0 %copy-start.5 = (pred[1024,8]{1,0:T(8,128)(4,1)S(1)}, pred[1024,8]{1,0:T(8,128)(4,1)}, u32[]{:S(2)}) copy-start(pred[1024,8]{1,0:T(8,128)(4,1)} %copy-done.4) | copy-start | bytes 24580
  12.9 61.1 %all-to-all-start = ((bf16[32,2,128]{2,1,0:T(2,128)(2,1)}), bf16[32,2,128]{2,1,0:T(2,128)(2,1)S(1)}, u32[]{:S(2)}, u32[]{:S(2)}) async-start(bf16[32,2,128]{2,1,0:T(2,128)(2,1)} %reshape.100), calls=%async_computation | async-start | bytes 32768 | tf_op jit(solution)/shard_map/all_to_all | solution.py:61
  46.3 33.5 %copy-start.6 = (s32[32,4]{0,1:T(4,128)S(1)}, s32[32,4]{0,1:T(4,128)}, u32[]{:S(2)}) copy-start(s32[32,4]{0,1:T(4,128)} %param.9) | copy-start | bytes 1540
  74.0 21.5 %all-to-all-start.1 = ((bf16[32,32,1,256]{3,1,2,0:T(8,128)(2,1)}), bf16[32,32,1,256]{3,1,2,0:T(8,128)(2,1)S(1)}, u32[]{:S(2)}, u32[]{:S(2)}) async-start(bf16[32,32,1,256]{3,1,2,0:T(8,128)(2,1)} %constant_dynamic-update-slice_fusion), calls=%async_computation.1 | async-start | bytes 1048576 | tf_op jit(solution)/shard_map/all_to_all | solution.py:53
  101.6 7.4 %copy-start.1 = (bf16[32,32,1,256]{1,0,3,2:T(8,128)(2,1)S(1)}, bf16[32,32,1,256]{1,0,3,2:T(8,128)(2,1)}, u32[]{:S(2)}) copy-start(bf16[32,32,1,256]{1,0,3,2:T(8,128)(2,1)} %copy.70) | copy-start | bytes 1572868
  104.6 5.1 %collective-permute-start = (f32[1,4,32]{2,1,0:T(4,128)S(1)}, f32[1,4,32]{2,1,0:T(4,128)S(1)}, u32[]{:S(2)}, u32[]{:S(2)}) collective-permute-start(f32[1,4,32]{2,1,0:T(4,128)S(1)} %get-tuple-element.63), channel_id=1, source_target_pairs={{0,4},{4,8},{8,12},{12,16},{16,20},{20,24},{24,28},{1,5},{5,9},{9,... | collective-permute-start | bytes 1544 | tf_op jit(solution)/shard_map/ppermute | solution.py:17
  107.7 5.5 %collective-permute-start.1 = (f32[1,4,32]{2,1,0:T(4,128)S(1)}, f32[1,4,32]{2,1,0:T(4,128)S(1)}, u32[]{:S(2)}, u32[]{:S(2)}) collective-permute-start(f32[1,4,32]{2,1,0:T(4,128)S(1)} %get-tuple-element.64), channel_id=1, source_target_pairs={{4,0},{8,4},{12,8},{16,12},{20,16},{24,20},{28,24},{5,1},{9,5},{13... | collective-permute-start | bytes 1544 | tf_op jit(solution)/shard_map/ppermute | solution.py:20
  109.7 10.5 %copy-start.2 = (f32[32,512]{1,0:T(8,128)S(1)}, f32[32,512]{1,0:T(8,128)}, u32[]{:S(2)}) copy-start(f32[32,512]{1,0:T(8,128)} %param.11) | copy-start | bytes 196612
  113.2 3.7 %collective-permute-start.2 = (f32[10,1,32]{2,1,0:T(1,128)S(1)}, f32[10,1,32]{2,1,0:T(1,128)S(1)}, u32[]{:S(2)}, u32[]{:S(2)}) collective-permute-start(f32[10,1,32]{2,1,0:T(1,128)S(1)} %get-tuple-element.53), channel_id=1, source_target_pairs={{0,1},{1,2},{2,3},{4,5},{5,6},{6,7},{8,9},{9,10},{10,11},{12,13},{... | collective-permute-start | bytes 3848 | tf_op jit(solution)/shard_map/ppermute | solution.py:17
  114.5 4.4 %collective-permute-start.3 = (f32[10,1,32]{2,1,0:T(1,128)S(1)}, f32[10,1,32]{2,1,0:T(1,128)S(1)}, u32[]{:S(2)}, u32[]{:S(2)}) collective-permute-start(f32[10,1,32]{2,1,0:T(1,128)S(1)} %get-tuple-element.54), channel_id=1, source_target_pairs={{1,0},{2,1},{3,2},{5,4},{6,5},{7,6},{9,8},{10,9},{11,10},{13,12},{... | collective-permute-start | bytes 3848 | tf_op jit(solution)/shard_map/ppermute | solution.py:20
  164.6 5.7 %collective-permute-start.4 = (f32[1,4,32]{2,1,0:T(4,128)S(1)}, f32[1,4,32]{2,1,0:T(4,128)S(1)}, u32[]{:S(2)}, u32[]{:S(2)}) collective-permute-start(f32[1,4,32]{2,1,0:T(4,128)S(1)} %get-tuple-element.57), channel_id=1, source_target_pairs={{0,4},{4,8},{8,12},{12,16},{16,20},{20,24},{24,28},{1,5},{5,9},{9,... | collective-permute-start | bytes 1544 | tf_op jit(solution)/shard_map/ppermute | solution.py:17
  169.0 5.5 %collective-permute-start.5 = (f32[1,4,32]{2,1,0:T(4,128)S(1)}, f32[1,4,32]{2,1,0:T(4,128)S(1)}, u32[]{:S(2)}, u32[]{:S(2)}) collective-permute-start(f32[1,4,32]{2,1,0:T(4,128)S(1)} %get-tuple-element.58), channel_id=1, source_target_pairs={{4,0},{8,4},{12,8},{16,12},{20,16},{24,20},{28,24},{5,1},{9,5},{13... | collective-permute-start | bytes 1544 | tf_op jit(solution)/shard_map/ppermute | solution.py:20
  174.5 3.5 %collective-permute-start.6 = (f32[10,1,32]{2,1,0:T(1,128)S(1)}, f32[10,1,32]{2,1,0:T(1,128)S(1)}, u32[]{:S(2)}, u32[]{:S(2)}) collective-permute-start(f32[10,1,32]{2,1,0:T(1,128)S(1)} %get-tuple-element.51), channel_id=1, source_target_pairs={{0,1},{1,2},{2,3},{4,5},{5,6},{6,7},{8,9},{9,10},{10,11},{12,13},{... | collective-permute-start | bytes 3848 | tf_op jit(solution)/shard_map/ppermute | solution.py:17
  175.8 3.7 %collective-permute-start.7 = (f32[10,1,32]{2,1,0:T(1,128)S(1)}, f32[10,1,32]{2,1,0:T(1,128)S(1)}, u32[]{:S(2)}, u32[]{:S(2)}) collective-permute-start(f32[10,1,32]{2,1,0:T(1,128)S(1)} %get-tuple-element.52), channel_id=1, source_target_pairs={{1,0},{2,1},{3,2},{5,4},{6,5},{7,6},{9,8},{10,9},{11,10},{13,12},{... | collective-permute-start | bytes 3848 | tf_op jit(solution)/shard_map/ppermute | solution.py:20
  229.8 5.7 %collective-permute-start.8 = (f32[1,4,32]{2,1,0:T(4,128)S(1)}, f32[1,4,32]{2,1,0:T(4,128)S(1)}, u32[]{:S(2)}, u32[]{:S(2)}) collective-permute-start(f32[1,4,32]{2,1,0:T(4,128)S(1)} %get-tuple-element.55), channel_id=1, source_target_pairs={{0,4},{4,8},{8,12},{12,16},{16,20},{20,24},{24,28},{1,5},{5,9},{9,... | collective-permute-start | bytes 1544 | tf_op jit(solution)/shard_map/ppermute | solution.py:17
  234.2 5.5 %collective-permute-start.9 = (f32[1,4,32]{2,1,0:T(4,128)S(1)}, f32[1,4,32]{2,1,0:T(4,128)S(1)}, u32[]{:S(2)}, u32[]{:S(2)}) collective-permute-start(f32[1,4,32]{2,1,0:T(4,128)S(1)} %get-tuple-element.56), channel_id=1, source_target_pairs={{4,0},{8,4},{12,8},{16,12},{20,16},{24,20},{28,24},{5,1},{9,5},{13... | collective-permute-start | bytes 1544 | tf_op jit(solution)/shard_map/ppermute | solution.py:20
  239.7 3.5 %collective-permute-start.10 = (f32[10,1,32]{2,1,0:T(1,128)S(1)}, f32[10,1,32]{2,1,0:T(1,128)S(1)}, u32[]{:S(2)}, u32[]{:S(2)}) collective-permute-start(f32[10,1,32]{2,1,0:T(1,128)S(1)} %get-tuple-element.49), channel_id=1, source_target_pairs={{0,1},{1,2},{2,3},{4,5},{5,6},{6,7},{8,9},{9,10},{10,11},{12,13},{... | collective-permute-start | bytes 3848 | tf_op jit(solution)/shard_map/ppermute | solution.py:17
  241.0 3.8 %collective-permute-start.11 = (f32[10,1,32]{2,1,0:T(1,128)S(1)}, f32[10,1,32]{2,1,0:T(1,128)S(1)}, u32[]{:S(2)}, u32[]{:S(2)}) collective-permute-start(f32[10,1,32]{2,1,0:T(1,128)S(1)} %get-tuple-element.50), channel_id=1, source_target_pairs={{1,0},{2,1},{3,2},{5,4},{6,5},{7,6},{9,8},{10,9},{11,10},{13,12},{... | collective-permute-start | bytes 3848 | tf_op jit(solution)/shard_map/ppermute | solution.py:20
